TPU v7x, 32 devices: a whole 2x2x4 slice. The times are simulated.
32 devices in a mesh: outer: 8 (over z, core), inner: 4 (over y, x).
Axes of the slice: x: 2, y: 2, z: 4, core: 2. Of those that a mesh axis runs over, the one named last changes fastest.
Arguments:
- leaf_blocks: float32 [32, 512, 512], P(('outer', 'inner')), as said below
- leaf_bases: float32 [32, 512, 256], P(('outer', 'inner'))
- local_gens: float32 [32, 2, 256, 256], P(('outer', 'inner'))
- chain_gens: float32 [64, 2, 256, 256], P(('outer', 'inner')), as said below
- node_ranks: int32 [3, 32], replicated, may hold values from 192 to 256, as said below
Outputs:
- local_reduced: float32 [32, 256, 256], P(('outer', 'inner'))
- chain_reduced: float32 [64, 256, 256], P(('outer', 'inner'))
- top_factor: float32 [16384, 512], P(('outer', 'inner'))
Inputs may be any that keep to these rules, and one draw needn't show every extreme that they name: `node_ranks`: ranks of all tree levels, entry [v, k] read for k < 32 >> v; both ends of the range occur in every draw. `leaf_blocks`: each leaf block is symmetric positive definite. Rows of chain_gens that belong to the same node are equal on all devices below that node.
All inputs are finite; a program needn't handle non-finite values.
Results may differ from a plain program's by a relative error of at most 0.00017.
Values sent between devices are 32-bit elements; how exact they have to be, the bound alone decides.
A program may use at most 128 MiB of HBM per device.

v0:
```python
import functools

import jax
import jax.numpy as jnp
from jax import lax
from jax.experimental import pallas as pl
from jax.experimental.pallas import tpu as pltpu
from jax.sharding import PartitionSpec as P

LANES = 128
SUB = 8
PANEL = 32
HIGH = lax.Precision.HIGHEST


def dot(a, b, dims=((1,), (0,))):
    return lax.dot_general(a, b, (dims, ((), ())), precision=HIGH, preferred_element_type=jnp.float32)


NT = ((1,), (1,))
TN = ((0,), (0,))


def thirds(x):
    a = x.astype(jnp.bfloat16)
    x = x - a.astype(jnp.float32)
    b = x.astype(jnp.bfloat16)
    return a, b, (x - b.astype(jnp.float32)).astype(jnp.bfloat16)


def bdot(a, b):
    return jnp.dot(a, b, preferred_element_type=jnp.float32)


def iota(shape, axis):
    return lax.broadcasted_iota(jnp.int32, shape, axis)


def row_of(x, j):
    return jnp.broadcast_to(x[j : j + 1, :], x.shape)


def col_of(x, c):
    return jnp.broadcast_to(x[:, c : c + 1], x.shape)


def eliminate(a_ref, keep_ref=None, reverse=False):
    n = a_ref.shape[0]
    tiles = n // LANES
    groups = PANEL // SUB
    sub = iota((SUB, LANES), 0)
    lane = iota((SUB, LANES), 1)
    wide = iota((n, LANES), 1)

    def order(count):
        return range(count - 1, -1, -1) if reverse else range(count)

    def tile_step(step, carry):
        h = tiles - 1 - step if reverse else step
        own_at = pl.multiple_of(h * LANES, LANES)
        spots = [own_at] + [pl.multiple_of(lax.rem(h + t, tiles) * LANES, LANES) for t in range(1, tiles)]
        for q in order(LANES // PANEL):
            base_row = pl.multiple_of(h * LANES + q * PANEL, PANEL)
            rows = [
                [a_ref[pl.ds(pl.multiple_of(base_row + g * SUB, SUB), SUB), pl.ds(spot, LANES)] for spot in spots]
                for g in range(groups)
            ]
            for s in order(groups):
                c0 = q * PANEL + s * SUB
                cols = [col_of(rows[s][0], c0 + j) for j in range(SUB)]
                other = {g: [col_of(rows[g][0], c0 + j) for j in range(SUB)] for g in range(groups) if g != s}
                piv = list(rows[s])
                kept = [jnp.zeros((SUB, LANES), jnp.float32) for _ in spots]
                left = list(order(SUB))
                inv = 1.0 / row_of(cols[left[0]], left[0])
                while left:
                    j = left.pop(0)
                    here = lane == c0 + j
                    at = sub == j
                    lines = [row_of(x, j) for x in piv]
                    if keep_ref is not None:
                        root = lax.rsqrt(row_of(cols[j], j))
                        kept = [jnp.where(at, x * root, k) for x, k in zip(lines, kept)]
                    mult = jnp.where(at, -1.0, cols[j])
                    now = inv
                    if left:
                        i = left[0]
                        cross = row_of(cols[i], j)
                        inv = 1.0 / (row_of(cols[i], i) - (cross * now) * row_of(cols[j], i))
                    lines = [jnp.where(here, 1.0, lines[0])] + lines[1:]
                    bases = [jnp.where(at | here, 0.0, piv[0])] + [jnp.where(at, 0.0, x) for x in piv[1:]]
                    piv = [y - mult * (x * now) for x, y in zip(lines, bases)]
                    for i in left:
                        cols[i] = jnp.where(at, 0.0, cols[i]) - mult * (row_of(cols[i], j) * now)
                rows[s] = piv
                if keep_ref is not None:
                    for spot, k in zip(spots, kept):
                        keep_ref[pl.ds(pl.multiple_of(base_row + s * SUB, SUB), SUB), pl.ds(spot, LANES)] = k
                spread = [[row_of(x, j) for j in range(SUB)] for x in piv]
                inside = (lane >= c0) & (lane < c0 + SUB)
                for g, mult in other.items():
                    new = list(rows[g])
                    new[0] = jnp.where(inside, 0.0, new[0])
                    for j in range(SUB):
                        new = [x - mult[j] * y[j] for x, y in zip(new, spread)]
                    rows[g] = new
            in_panel = (wide >= q * PANEL) & (wide < (q + 1) * PANEL)
            own = a_ref[:, pl.ds(own_at, LANES)]
            a_ref[:, pl.ds(own_at, LANES)] = jnp.where(in_panel, 0.0, own)
            l1, l2, l3 = thirds(jnp.where(in_panel, own, 0.0))
            l12 = jnp.concatenate([l1, l2], axis=1)
            l31 = jnp.concatenate([l3, l1], axis=1)
            for t, spot in enumerate(spots):
                r1, r2, r3 = thirds(jnp.concatenate([rows[g][t] for g in range(groups)], axis=0))
                above = jnp.zeros((q * PANEL, LANES), jnp.bfloat16)
                below = jnp.zeros((LANES - (q + 1) * PANEL, LANES), jnp.bfloat16)

                def tall(x, y):
                    parts = [above, x, below, above, y, below]
                    return jnp.concatenate([p for p in parts if p.shape[0]], axis=0)

                change = bdot(l12, tall(r1, r1)) + (bdot(l12, tall(r2, r2)) + bdot(l31, tall(r1, r3)))
                a_ref[:, pl.ds(spot, LANES)] = a_ref[:, pl.ds(spot, LANES)] - change
            for g in range(groups):
                for spot, x in zip(spots, rows[g]):
                    a_ref[pl.ds(pl.multiple_of(base_row + g * SUB, SUB), SUB), pl.ds(spot, LANES)] = x
        return carry

    lax.fori_loop(0, tiles, tile_step, 0)


def unit_rest(n, rank):
    return jnp.where((iota((n, n), 0) == iota((n, n), 1)) & (iota((n, n), 0) >= rank), 1.0, 0.0)


def both(n, rank_row, rank_col, x):
    return jnp.where((iota((n, n), 0) < rank_row) & (iota((n, n), 1) < rank_col), x, 0.0)


def place():
    return lax.axis_index("outer") * lax.axis_size("inner") + lax.axis_index("inner")


def leaf_kernel(rank_ref, m_ref, v_ref, g_ref, a_ref):
    n = g_ref.shape[0]
    rank = rank_ref[0, place()]
    keep = iota((n, n), 1) < rank
    v1 = jnp.where(keep, v_ref[:n, :], 0.0)
    v2 = jnp.where(keep, v_ref[n:, :], 0.0)
    a_ref[...] = m_ref[n:, n:]
    eliminate(a_ref)
    m12 = m_ref[:n, n:]
    w = dot(m12, a_ref[...])
    t = dot(a_ref[...], v2)
    a_ref[...] = m_ref[:n, :n] - dot(w, m12, NT)
    y = v1 - dot(w, v2)
    eliminate(a_ref)
    g_ref[...] = dot(v2, t, TN) + dot(y, dot(a_ref[...], y), TN) + unit_rest(n, rank)


def invert_kernel(depth, rank_ref, g_ref, l_ref, a_ref):
    n = g_ref.shape[0]
    rank = rank_ref[depth, jnp.right_shift(place(), depth)]
    a_ref[...] = g_ref[...]
    eliminate(a_ref)
    l_ref[...] = both(n, rank, rank, a_ref[...])


def last_kernel(depth, rank_ref, g_ref, l_ref, e_ref, a_ref):
    n = g_ref.shape[0]
    rank = rank_ref[depth, jnp.right_shift(place(), depth)]
    a_ref[...] = g_ref[...]
    eliminate(a_ref, e_ref, reverse=True)
    l_ref[...] = both(n, rank, rank, a_ref[...])


def merge_kernel(depth, rank_ref, l_ref, gy_ref, mine_ref, theirs_ref, g_ref, a_ref):
    n = g_ref.shape[0]
    node = jnp.right_shift(place(), depth)
    rx, ry = rank_ref[depth, node], rank_ref[depth, jnp.bitwise_xor(node, 1)]
    rp = rank_ref[depth + 1, jnp.right_shift(node, 1)]
    couple = both(n, rx, ry, mine_ref[1] + theirs_ref[1].T)
    px = both(n, rx, rp, mine_ref[0])
    py = both(n, ry, rp, theirs_ref[0])
    gy = gy_ref[...]
    w = dot(couple, gy)
    a_ref[...] = l_ref[...] + unit_rest(n, rx) - dot(w, couple, NT)
    y = px - dot(w, py)
    t = dot(py, dot(gy, py), TN)
    eliminate(a_ref)
    g_ref[...] = t + dot(y, dot(a_ref[...], y), TN) + unit_rest(n, rp)


def top_kernel(depth, rank_ref, l_ref, e_ref, lo_ref, eo_ref, c_ref, co_ref, f_ref, a_ref, keep_ref):
    n = l_ref.shape[0]
    pos = lax.axis_index("outer")
    first = jnp.bitwise_and(pos, 1) == 0
    node = jnp.bitwise_and(pos, -2)
    ra, rb = rank_ref[depth, node], rank_ref[depth, node + 1]
    row, col = iota((n, n), 0), iota((n, n), 1)
    pick = jnp.where(first, 1, 0) + jnp.zeros((n, n), jnp.int32) > 0
    ca = jnp.where(pick, c_ref[...], co_ref[...])
    cb = jnp.where(pick, co_ref[...], c_ref[...])
    lb = jnp.where(pick, lo_ref[...], l_ref[...])
    e = jnp.where(pick, e_ref[...], eo_ref[...])
    couple = both(n, ra, rb, ca + cb.T)
    f21 = dot(couple, jnp.where(row >= col, e, 0.0), ((0,), (1,)))
    a_ref[...] = lb + unit_rest(n, rb) - dot(f21, f21, NT)
    eliminate(a_ref, keep_ref)
    upper = jnp.where(row < col, e, 0.0) + jnp.where(row == col, 1.0 / jnp.where(row == col, e, 1.0), 0.0)
    f_ref[:n, :n] = upper.T
    f_ref[:n, n:] = jnp.zeros((n, n), jnp.float32)
    f_ref[n:, :n] = f21
    f_ref[n:, n:] = jnp.where(row <= col, keep_ref[...], 0.0).T


def call(kernel, name, outs, n, ranks, *arrays, keep=False):
    vmem = pl.BlockSpec(memory_space=pltpu.VMEM)
    square = pltpu.VMEM((n, n), jnp.float32)
    return pl.pallas_call(
        kernel,
        name=name,
        out_shape=[jax.ShapeDtypeStruct(shape, jnp.float32) for shape in outs],
        in_specs=[pl.BlockSpec(memory_space=pltpu.SMEM)] + [vmem] * len(arrays),
        out_specs=[vmem] * len(outs),
        scratch_shapes=[square] * (2 if keep else 1),
        cost_estimate=pl.CostEstimate(flops=4 * 10**9, bytes_accessed=4 * 10**6, transcendentals=0),
    )(ranks, *arrays)


def partner(x, axis, bit):
    return lax.ppermute(x, axis, [(i, i ^ 1 << bit) for i in range(lax.axis_size(axis))])


def body(leaf_blocks, leaf_bases, local_gens, chain_gens, node_ranks):
    n = leaf_bases.shape[2]
    in_levels = chain_gens.shape[0]
    square = (n, n)
    gens = [local_gens[0]] + [chain_gens[d] for d in range(in_levels)]
    others = [partner(gens[d], "inner", d) for d in range(in_levels)]
    couple = gens[in_levels][1]
    other_couple = partner(couple, "outer", 0)
    g = call(leaf_kernel, "leaf", [square], n, node_ranks, leaf_blocks[0], leaf_bases[0])[0]
    reduced = []
    for depth in range(in_levels):
        g_other = partner(g, "inner", depth)
        mine = call(functools.partial(invert_kernel, depth), "invert", [square], n, node_ranks, g)[0]
        reduced.append(mine)
        merge = functools.partial(merge_kernel, depth)
        g = call(merge, "merge", [square], n, node_ranks, mine, g_other, gens[depth], others[depth])[0]
    last = functools.partial(last_kernel, in_levels)
    mine, roots = call(last, "last", [square, square], n, node_ranks, g)
    reduced.append(mine)
    other_mine, other_roots = partner((mine, roots), "outer", 0)
    top = functools.partial(top_kernel, in_levels)
    arrays = (mine, roots, other_mine, other_roots, couple, other_couple)
    factor = call(top, "top", [(2 * n, 2 * n)], n, node_ranks, *arrays, keep=True)[0]
    return (reduced[0][None], jnp.stack(reduced[1:], axis=0), factor)


def solution(mesh):
    return jax.shard_map(
        body,
        mesh=mesh,
        in_specs=(
            P(("outer", "inner"), None, None),
            P(("outer", "inner"), None, None),
            P(("outer", "inner"), None, None, None),
            P(("outer", "inner"), None, None, None),
            P(),
        ),
        out_specs=(
            P(("outer", "inner"), None, None),
            P(("outer", "inner"), None, None),
            P(("outer", "inner"), None),
        ),
        check_vma=False,
    )
```

profile of v0, /device:TPU:0, one launch (start us, length us, event | category | flops | bytes accessed | tf_op | source)
XLA Modules:
  0.0 124.0 jit_solution(14887873149956490143)
XLA Ops:
  0.6 0.0 copy-start.4
  0.6 0.0 copy-start
  0.7 25.5 %leaf.1.g_ref = f32[256,256]{1,0:T(8,128)} custom-call(s32[3,32]{1,0:T(4,128)} %rank_ref.13, f32[512,512]{1,0:T(8,128)} %bitcast.12, f32[512,256]{1,0:T(8,128)} %bitcast.13), custom_call_target="tpu_custom_call" | custom-call | flops 4000000000 | bytes 4000000 | tf_op jit(solution)/shard_map/leaf/pallas_call | solution.py:220
  26.2 3.0 %collective-permute-start = (f32[256,256]{1,0:T(8,128)}, f32[256,256]{1,0:T(8,128)}, u32[]{:S(2)}, u32[]{:S(2)}) collective-permute-start(f32[256,256]{1,0:T(8,128)} %leaf.1.g_ref), channel_id=1, source_target_pairs={{0,1},{1,0},{2,3},{3,2},{4,5},{5,4},{6,7},{7,6},{8,9},{9,8},{10,11... | collective-permute-start | bytes 786440 | tf_op jit(solution)/shard_map/ppermute | solution.py:232
  29.1 0.0 copy-done.4
  29.2 0.0 collective-permute-start.1
  29.2 0.0 copy-done
  29.2 0.0 copy-start.1
  29.2 2.1 %collective-permute-start.3 = (f32[2,256,256]{2,1,0:T(8,128)S(1)}, f32[2,256,256]{2,1,0:T(8,128)S(1)}, u32[]{:S(2)}, u32[]{:S(2)}) collective-permute-start(f32[2,256,256]{2,1,0:T(8,128)S(1)} %slice_bitcast_fusion.mine_ref), channel_id=1, source_target_pairs={{0,2},{1,3},{2,0},{3,1},{4,6},{5,7},{6,4},{7,5},{8,10},{9,11},{10,... | collective-permute-start | bytes 1572872 | tf_op jit(solution)/shard_map/ppermute | solution.py:232
  31.3 0.0 copy-start.2
  31.4 0.1 collective-permute-start.6
  31.4 12.3 %invert.2.l_ref = f32[256,256]{1,0:T(8,128)} custom-call(s32[3,32]{1,0:T(4,128)} %rank_ref.13, f32[256,256]{1,0:T(8,128)} %leaf.1.g_ref), custom_call_target="tpu_custom_call" | custom-call | flops 4000000000 | bytes 4000000 | tf_op jit(solution)/shard_map/invert/pallas_call | solution.py:220
  43.7 0.0 copy-done.1
  43.7 0.0 copy-done.2
  43.7 0.0 collective-permute-done.gy_ref
  43.7 3.2 %collective-permute-done.1.theirs_ref = f32[2,256,256]{2,1,0:T(8,128)S(1)} collective-permute-done((f32[2,256,256]{2,1,0:T(8,128)S(1)}, f32[2,256,256]{2,1,0:T(8,128)S(1)}, u32[]{:S(2)}, u32[]{:S(2)}) %collective-permute-start.1) | collective-permute-done | bytes 524320 | tf_op jit(solution)/shard_map/ppermute | solution.py:232
  46.9 0.0 copy-start.6
  46.9 0.8 copy-done.6
  47.7 15.3 %merge.2.g_ref = f32[256,256]{1,0:T(8,128)} custom-call(s32[3,32]{1,0:T(4,128)} %rank_ref.13, f32[256,256]{1,0:T(8,128)} %invert.2.l_ref, f32[256,256]{1,0:T(8,128)} %collective-permute-done.gy_ref, f32[2,256,256]{2,1,0:T(8,128)} %bitcast.14, f32[2,256,256]{2,1,0:T(8,128)} %copy-done.6), custom_call_target="tpu_custom_call" | custom-call | flops 4000000000 | bytes 4000000 | tf_op jit(solution)/shard_map/merge/pallas_call | solution.py:220
  63.0 1.8 %collective-permute-start.2 = (f32[256,256]{1,0:T(8,128)}, f32[256,256]{1,0:T(8,128)S(1)}, u32[]{:S(2)}, u32[]{:S(2)}) collective-permute-start(f32[256,256]{1,0:T(8,128)} %merge.2.g_ref), channel_id=1, source_target_pairs={{0,2},{1,3},{2,0},{3,1},{4,6},{5,7},{6,4},{7,5},{8,10},{9,11},{10,... | collective-permute-start | bytes 786440 | tf_op jit(solution)/shard_map/ppermute | solution.py:232
  64.7 12.1 %invert.3.l_ref = f32[256,256]{1,0:T(8,128)} custom-call(s32[3,32]{1,0:T(4,128)} %rank_ref.13, f32[256,256]{1,0:T(8,128)} %merge.2.g_ref), custom_call_target="tpu_custom_call" | custom-call | flops 4000000000 | bytes 4000000 | tf_op jit(solution)/shard_map/invert/pallas_call | solution.py:220
  76.8 0.0 collective-permute-done.3.theirs_ref
  76.8 0.0 copy-start.5
  76.9 0.0 collective-permute-done.2.gy_ref
  76.9 0.8 copy-done.5
  77.6 0.0 copy-start.10
  77.6 0.7 copy-done.10
  78.3 15.5 %merge.3.g_ref = f32[256,256]{1,0:T(8,128)} custom-call(s32[3,32]{1,0:T(4,128)} %rank_ref.13, f32[256,256]{1,0:T(8,128)} %invert.3.l_ref, f32[256,256]{1,0:T(8,128)} %copy-done.10, f32[2,256,256]{2,1,0:T(8,128)} %copy-done.1, f32[2,256,256]{2,1,0:T(8,128)} %copy-done.5), custom_call_target="tpu_custom_call" | custom-call | flops 4000000000 | bytes 4000000 | tf_op jit(solution)/shard_map/merge/pallas_call | solution.py:220
  93.9 0.0 copy-start.3
  93.9 12.2 %last.1 = (f32[256,256]{1,0:T(8,128)}, f32[256,256]{1,0:T(8,128)}) custom-call(s32[3,32]{1,0:T(4,128)} %rank_ref.13, f32[256,256]{1,0:T(8,128)} %merge.3.g_ref), custom_call_target="tpu_custom_call" | custom-call | flops 4000000000 | bytes 4000000 | tf_op jit(solution)/shard_map/last/pallas_call | solution.py:220
  106.0 0.0 collective-permute-start.4
  106.0 0.5 collective-permute-start.5
  106.5 0.0 copy-done.3
  106.5 1.8 %pad_maximum_fusion = f32[2,256,256]{2,1,0:T(8,128)} fusion(f32[1,256,256]{2,1,0:T(8,128)} %bitcast.11, f32[1,256,256]{2,1,0:T(8,128)S(1)} %bitcast.10), kind=kLoop, calls=%fused_computation | loop fusion | flops 131072 | bytes 1048576 | tf_op jit(solution)/shard_map/stack | solution.py:258
  108.3 0.0 collective-permute-done.6.co_ref
  108.3 0.0 copy-start.7
  108.3 0.0 collective-permute-done.4.lo_ref
  108.3 0.0 copy-start.8
  108.3 0.0 collective-permute-done.5.eo_ref
  108.3 0.7 copy-done.7
  109.0 0.1 copy-done.8
  109.1 0.0 copy-start.9
  109.1 0.7 copy-done.9
  109.8 14.1 %top.1 = f32[512,512]{1,0:T(8,128)} custom-call(s32[3,32]{1,0:T(4,128)} %rank_ref.13, f32[256,256]{1,0:T(8,128)} %get-tuple-element.5.l_ref, f32[256,256]{1,0:T(8,128)} %get-tuple-element.6.e_ref, f32[256,256]{1,0:T(8,128)} %copy-done.8, f32[256,256]{1,0:T(8,128)} %copy-done.9, f32[256,256]{1,0:T(8,128)} %copy-done.2, f32[256,256]{1,0:T(8,128)} %copy-done.7), custom_call_target="tpu_custom_call" | custom-call | flops 4000000000 | bytes 4000000 | tf_op jit(solution)/shard_map/top/pallas_call | solution.py:220
  (2 shorter events, 0.1 us)
Async XLA Ops:
  0.6 28.5 %copy-start.4 = (f32[1,2,256,256]{3,2,1,0:T(8,128)S(1)}, f32[1,2,256,256]{3,2,1,0:T(8,128)}, u32[]{:S(2)}) copy-start(f32[1,2,256,256]{3,2,1,0:T(8,128)} %param.7) | copy-start | bytes 1572868
  0.6 28.5 %copy-start = (f32[2,2,256,256]{3,2,1,0:T(8,128)S(1)}, f32[2,2,256,256]{3,2,1,0:T(8,128)}, u32[]{:S(2)}) copy-start(f32[2,2,256,256]{3,2,1,0:T(8,128)} %param.8) | copy-start | bytes 3145732
  26.2 17.5 %collective-permute-start = (f32[256,256]{1,0:T(8,128)}, f32[256,256]{1,0:T(8,128)}, u32[]{:S(2)}, u32[]{:S(2)}) collective-permute-start(f32[256,256]{1,0:T(8,128)} %leaf.1.g_ref), channel_id=1, source_target_pairs={{0,1},{1,0},{2,3},{3,2},{4,5},{5,4},{6,7},{7,6},{8,9},{9,8},{10,11... | collective-permute-start | bytes 786440 | tf_op jit(solution)/shard_map/ppermute | solution.py:232
  29.2 17.7 %collective-permute-start.1 = (f32[2,256,256]{2,1,0:T(8,128)S(1)}, f32[2,256,256]{2,1,0:T(8,128)S(1)}, u32[]{:S(2)}, u32[]{:S(2)}) collective-permute-start(f32[2,256,256]{2,1,0:T(8,128)S(1)} %bitcast.15), channel_id=1, source_target_pairs={{0,1},{1,0},{2,3},{3,2},{4,5},{5,4},{6,7},{7,6},{8,9},{9,8},{10,11... | collective-permute-start | bytes 1572872 | tf_op jit(solution)/shard_map/ppermute | solution.py:232
  29.2 14.5 %copy-start.1 = (f32[2,256,256]{2,1,0:T(8,128)}, f32[2,256,256]{2,1,0:T(8,128)S(1)}, u32[]{:S(2)}) copy-start(f32[2,256,256]{2,1,0:T(8,128)S(1)} %slice_bitcast_fusion.mine_ref) | copy-start | bytes 1572868
  29.2 47.6 %collective-permute-start.3 = (f32[2,256,256]{2,1,0:T(8,128)S(1)}, f32[2,256,256]{2,1,0:T(8,128)S(1)}, u32[]{:S(2)}, u32[]{:S(2)}) collective-permute-start(f32[2,256,256]{2,1,0:T(8,128)S(1)} %slice_bitcast_fusion.mine_ref), channel_id=1, source_target_pairs={{0,2},{1,3},{2,0},{3,1},{4,6},{5,7},{6,4},{7,5},{8,10},{9,11},{10,... | collective-permute-start | bytes 1572872 | tf_op jit(solution)/shard_map/ppermute | solution.py:232
  31.3 12.4 %copy-start.2 = (f32[256,256]{1,0:T(8,128)}, f32[256,256]{1,0:T(8,128)S(1)}, u32[]{:S(2)}) copy-start(f32[256,256]{1,0:T(8,128)S(1)} %slice_bitcast_fusion.1.c_ref) | copy-start | bytes 786436
  31.4 77.0 %collective-permute-start.6 = (f32[256,256]{1,0:T(8,128)S(1)}, f32[256,256]{1,0:T(8,128)S(1)}, u32[]{:S(2)}, u32[]{:S(2)}) collective-permute-start(f32[256,256]{1,0:T(8,128)S(1)} %slice_bitcast_fusion.1.c_ref), channel_id=1, source_target_pairs={{0,4},{4,0},{8,12},{12,8},{16,20},{20,16},{24,28},{28,24},{1,5},{5... | collective-permute-start | bytes 786440 | tf_op jit(solution)/shard_map/ppermute | solution.py:232
  46.9 0.8 copy-start.6
  63.0 13.9 %collective-permute-start.2 = (f32[256,256]{1,0:T(8,128)}, f32[256,256]{1,0:T(8,128)S(1)}, u32[]{:S(2)}, u32[]{:S(2)}) collective-permute-start(f32[256,256]{1,0:T(8,128)} %merge.2.g_ref), channel_id=1, source_target_pairs={{0,2},{1,3},{2,0},{3,1},{4,6},{5,7},{6,4},{7,5},{8,10},{9,11},{10,... | collective-permute-start | bytes 786440 | tf_op jit(solution)/shard_map/ppermute | solution.py:232
  76.8 0.8 copy-start.5
  77.6 0.7 copy-start.10
  93.9 12.7 %copy-start.3 = (f32[256,256]{1,0:T(8,128)S(1)}, f32[256,256]{1,0:T(8,128)}, u32[]{:S(2)}) copy-start(f32[256,256]{1,0:T(8,128)} %invert.3.l_ref) | copy-start | bytes 786436
  106.0 2.3 %collective-permute-start.4 = (f32[256,256]{1,0:T(8,128)}, f32[256,256]{1,0:T(8,128)S(1)}, u32[]{:S(2)}, u32[]{:S(2)}) collective-permute-start(f32[256,256]{1,0:T(8,128)} %get-tuple-element.5.l_ref), channel_id=1, source_target_pairs={{0,4},{4,0},{8,12},{12,8},{16,20},{20,16},{24,28},{28,24},{1,5},{5... | collective-permute-start | bytes 786440 | tf_op jit(solution)/shard_map/ppermute | solution.py:232
  106.0 2.3 %collective-permute-start.5 = (f32[256,256]{1,0:T(8,128)}, f32[256,256]{1,0:T(8,128)S(1)}, u32[]{:S(2)}, u32[]{:S(2)}) collective-permute-start(f32[256,256]{1,0:T(8,128)} %get-tuple-element.6.e_ref), channel_id=1, source_target_pairs={{0,4},{4,0},{8,12},{12,8},{16,20},{20,16},{24,28},{28,24},{1,5},{5... | collective-permute-start | bytes 786440 | tf_op jit(solution)/shard_map/ppermute | solution.py:232
  108.3 0.7 copy-start.7
  108.3 0.8 copy-start.8
  109.1 0.7 copy-start.9
where the time goes:
time: 124 us
  Pallas kernels  107 us (86%)
  starting transfers between devices  7.45 us (6%)
  local copies, waits for them, and re-layouts  3.84 us (3%)
  waiting for transfers between devices  3.17 us (3%)
  other arithmetic  1.78 us (1%)
    pallas_call x7, Pallas kernels, call(): pl.pallas_call(kernel, name=name, out_shape=[jax.ShapeDtypeStruct(shape,...  107 us
    ppermute x7, starting transfers between devices, partner(): lax.ppermute(x, axis, [(i, i ^ 1 << bit) for i in range(lax.axis_size(axi...  7.45 us
    unnamed x22, local copies, waits for them, and re-layouts  3.79 us
    ppermute x7, waiting for transfers between devices, partner(): lax.ppermute(x, axis, [(i, i ^ 1 << bit) for i in range(lax.axis_size(axi...  3.17 us
  transfers between devices with their start and end apart: 7, of which 1 were waited for; matrix products, arithmetic and copies ran while one was open for 1% of the time, Pallas kernels for 54%

commit v1 on v0

--- a/solution.py
+++ b/solution.py
@@ -34,6 +34,12 @@
 
 def iota(shape, axis):
     return lax.broadcasted_iota(jnp.int32, shape, axis)
+
+
+def total(terms):
+    while len(terms) > 1:
+        terms = [a + b for a, b in zip(terms[::2], terms[1::2])]
+    return terms[0]
 
 
 def row_of(x, j):
@@ -59,12 +65,14 @@
         h = tiles - 1 - step if reverse else step
         own_at = pl.multiple_of(h * LANES, LANES)
         spots = [own_at] + [pl.multiple_of(lax.rem(h + t, tiles) * LANES, LANES) for t in range(1, tiles)]
-        for q in order(LANES // PANEL):
+        ahead = None
+        panels = list(order(LANES // PANEL))
+        for q in panels:
             base_row = pl.multiple_of(h * LANES + q * PANEL, PANEL)
             rows = [
                 [a_ref[pl.ds(pl.multiple_of(base_row + g * SUB, SUB), SUB), pl.ds(spot, LANES)] for spot in spots]
                 for g in range(groups)
-            ]
+            ] if ahead is None else ahead
             for s in order(groups):
                 c0 = q * PANEL + s * SUB
                 cols = [col_of(rows[s][0], c0 + j) for j in range(SUB)]
@@ -101,16 +109,9 @@
                 for g, mult in other.items():
                     new = list(rows[g])
                     new[0] = jnp.where(inside, 0.0, new[0])
-                    for j in range(SUB):
-                        new = [x - mult[j] * y[j] for x, y in zip(new, spread)]
-                    rows[g] = new
-            in_panel = (wide >= q * PANEL) & (wide < (q + 1) * PANEL)
-            own = a_ref[:, pl.ds(own_at, LANES)]
-            a_ref[:, pl.ds(own_at, LANES)] = jnp.where(in_panel, 0.0, own)
-            l1, l2, l3 = thirds(jnp.where(in_panel, own, 0.0))
-            l12 = jnp.concatenate([l1, l2], axis=1)
-            l31 = jnp.concatenate([l3, l1], axis=1)
-            for t, spot in enumerate(spots):
+                    rows[g] = [x - total([mult[j] * y[j] for j in range(SUB)]) for x, y in zip(new, spread)]
+            weights = []
+            for t in range(tiles):
                 r1, r2, r3 = thirds(jnp.concatenate([rows[g][t] for g in range(groups)], axis=0))
                 above = jnp.zeros((q * PANEL, LANES), jnp.bfloat16)
                 below = jnp.zeros((LANES - (q + 1) * PANEL, LANES), jnp.bfloat16)
@@ -119,8 +120,27 @@
                     parts = [above, x, below, above, y, below]
                     return jnp.concatenate([p for p in parts if p.shape[0]], axis=0)
 
-                change = bdot(l12, tall(r1, r1)) + (bdot(l12, tall(r2, r2)) + bdot(l31, tall(r1, r3)))
-                a_ref[:, pl.ds(spot, LANES)] = a_ref[:, pl.ds(spot, LANES)] - change
+                weights.append((tall(r1, r1), tall(r2, r2), tall(r1, r3)))
+
+            def updated(at, count):
+                inside = (wide[:count] >= q * PANEL) & (wide[:count] < (q + 1) * PANEL)
+                own = a_ref[pl.ds(at, count), pl.ds(own_at, LANES)]
+                l1, l2, l3 = thirds(jnp.where(inside, own, 0.0))
+                l12 = jnp.concatenate([l1, l2], axis=1)
+                l31 = jnp.concatenate([l3, l1], axis=1)
+                olds = [jnp.where(inside, 0.0, own)] + [a_ref[pl.ds(at, count), pl.ds(spot, LANES)] for spot in spots[1:]]
+                return [
+                    old - (bdot(l12, w11) + (bdot(l12, w22) + bdot(l31, w13)))
+                    for old, (w11, w22, w13) in zip(olds, weights)
+                ]
+
+            ahead = None
+            if q != panels[-1]:
+                onward = -PANEL if reverse else PANEL
+                block = updated(pl.multiple_of(base_row + onward, PANEL), PANEL)
+                ahead = [[x[g * SUB : (g + 1) * SUB] for x in block] for g in range(groups)]
+            for spot, x in zip(spots, updated(0, n)):
+                a_ref[:, pl.ds(spot, LANES)] = x
             for g in range(groups):
                 for spot, x in zip(spots, rows[g]):
                     a_ref[pl.ds(pl.multiple_of(base_row + g * SUB, SUB), SUB), pl.ds(spot, LANES)] = x

time: 124 us -> 119 us (0.960)
  Pallas kernels: 107 us -> 101 us
    pallas_call x7, Pallas kernels: 107 us -> 101 us  [call(): pl.pallas_call(kernel, name=name, out_shape=[jax.ShapeDtypeStruct(shape,...]
  transfers between devices with their start and end apart: 7 -> 7, of which waited for: 1 -> 1; matrix products, arithmetic and copies ran while one was open for 1% -> 2% of each run, Pallas kernels for 54% -> 54%
where the time goes in v1:
time: 119 us
  Pallas kernels  101 us (85%)
  starting transfers between devices  7.44 us (6%)
  waiting for transfers between devices  3.86 us (3%)
  local copies, waits for them, and re-layouts  3.84 us (3%)
  other arithmetic  1.78 us (1%)
    pallas_call x7, Pallas kernels, call(): pl.pallas_call(kernel, name=name, out_shape=[jax.ShapeDtypeStruct(shape,...  101 us
    ppermute x7, starting transfers between devices, partner(): lax.ppermute(x, axis, [(i, i ^ 1 << bit) for i in range(lax.axis_size(axi...  7.44 us
    ppermute x7, waiting for transfers between devices, partner(): lax.ppermute(x, axis, [(i, i ^ 1 << bit) for i in range(lax.axis_size(axi...  3.86 us
    unnamed x22, local copies, waits for them, and re-layouts  3.79 us
  transfers between devices with their start and end apart: 7, of which 1 were waited for; matrix products, arithmetic and copies ran while one was open for 2% of the time, Pallas kernels for 54%

profile of v1, /device:TPU:0, one launch (start us, length us, event | category | flops | bytes accessed | tf_op | source)
XLA Modules:
  0.0 119.0 jit_solution(15620689569094537060)
XLA Ops:
  0.6 0.0 copy-start.4
  0.6 0.0 copy-start
  0.7 24.1 %leaf.1.g_ref = f32[256,256]{1,0:T(8,128)} custom-call(s32[3,32]{1,0:T(4,128)} %rank_ref.13, f32[512,512]{1,0:T(8,128)} %bitcast.12, f32[512,256]{1,0:T(8,128)} %bitcast.13), custom_call_target="tpu_custom_call" | custom-call | flops 4000000000 | bytes 4000000 | tf_op jit(solution)/shard_map/leaf/pallas_call | solution.py:240
  24.8 3.0 %collective-permute-start = (f32[256,256]{1,0:T(8,128)}, f32[256,256]{1,0:T(8,128)}, u32[]{:S(2)}, u32[]{:S(2)}) collective-permute-start(f32[256,256]{1,0:T(8,128)} %leaf.1.g_ref), channel_id=1, source_target_pairs={{0,1},{1,0},{2,3},{3,2},{4,5},{5,4},{6,7},{7,6},{8,9},{9,8},{10,11... | collective-permute-start | bytes 786440 | tf_op jit(solution)/shard_map/ppermute | solution.py:252
  27.7 0.0 copy-done.4
  27.7 0.0 collective-permute-start.1
  27.7 0.0 copy-done
  27.8 0.0 copy-start.1
  27.8 2.1 %collective-permute-start.3 = (f32[2,256,256]{2,1,0:T(8,128)S(1)}, f32[2,256,256]{2,1,0:T(8,128)S(1)}, u32[]{:S(2)}, u32[]{:S(2)}) collective-permute-start(f32[2,256,256]{2,1,0:T(8,128)S(1)} %slice_bitcast_fusion.mine_ref), channel_id=1, source_target_pairs={{0,2},{1,3},{2,0},{3,1},{4,6},{5,7},{6,4},{7,5},{8,10},{9,11},{10,... | collective-permute-start | bytes 1572872 | tf_op jit(solution)/shard_map/ppermute | solution.py:252
  29.9 0.0 copy-start.2
  29.9 0.1 collective-permute-start.6
  30.0 11.6 %invert.2.l_ref = f32[256,256]{1,0:T(8,128)} custom-call(s32[3,32]{1,0:T(4,128)} %rank_ref.13, f32[256,256]{1,0:T(8,128)} %leaf.1.g_ref), custom_call_target="tpu_custom_call" | custom-call | flops 4000000000 | bytes 4000000 | tf_op jit(solution)/shard_map/invert/pallas_call | solution.py:240
  41.6 0.0 copy-done.1
  41.6 0.0 copy-done.2
  41.6 0.0 collective-permute-done.gy_ref
  41.6 3.8 %collective-permute-done.1.theirs_ref = f32[2,256,256]{2,1,0:T(8,128)S(1)} collective-permute-done((f32[2,256,256]{2,1,0:T(8,128)S(1)}, f32[2,256,256]{2,1,0:T(8,128)S(1)}, u32[]{:S(2)}, u32[]{:S(2)}) %collective-permute-start.1) | collective-permute-done | bytes 524320 | tf_op jit(solution)/shard_map/ppermute | solution.py:252
  45.5 0.0 copy-start.6
  45.5 0.8 copy-done.6
  46.3 14.6 %merge.2.g_ref = f32[256,256]{1,0:T(8,128)} custom-call(s32[3,32]{1,0:T(4,128)} %rank_ref.13, f32[256,256]{1,0:T(8,128)} %invert.2.l_ref, f32[256,256]{1,0:T(8,128)} %collective-permute-done.gy_ref, f32[2,256,256]{2,1,0:T(8,128)} %bitcast.14, f32[2,256,256]{2,1,0:T(8,128)} %copy-done.6), custom_call_target="tpu_custom_call" | custom-call | flops 4000000000 | bytes 4000000 | tf_op jit(solution)/shard_map/merge/pallas_call | solution.py:240
  60.9 1.8 %collective-permute-start.2 = (f32[256,256]{1,0:T(8,128)}, f32[256,256]{1,0:T(8,128)S(1)}, u32[]{:S(2)}, u32[]{:S(2)}) collective-permute-start(f32[256,256]{1,0:T(8,128)} %merge.2.g_ref), channel_id=1, source_target_pairs={{0,2},{1,3},{2,0},{3,1},{4,6},{5,7},{6,4},{7,5},{8,10},{9,11},{10,... | collective-permute-start | bytes 786440 | tf_op jit(solution)/shard_map/ppermute | solution.py:252
  62.6 11.4 %invert.3.l_ref = f32[256,256]{1,0:T(8,128)} custom-call(s32[3,32]{1,0:T(4,128)} %rank_ref.13, f32[256,256]{1,0:T(8,128)} %merge.2.g_ref), custom_call_target="tpu_custom_call" | custom-call | flops 4000000000 | bytes 4000000 | tf_op jit(solution)/shard_map/invert/pallas_call | solution.py:240
  74.1 0.0 collective-permute-done.3.theirs_ref
  74.1 0.0 copy-start.5
  74.1 0.0 collective-permute-done.2.gy_ref
  74.1 0.8 copy-done.5
  74.9 0.0 copy-start.10
  74.9 0.7 copy-done.10
  75.6 14.8 %merge.3.g_ref = f32[256,256]{1,0:T(8,128)} custom-call(s32[3,32]{1,0:T(4,128)} %rank_ref.13, f32[256,256]{1,0:T(8,128)} %invert.3.l_ref, f32[256,256]{1,0:T(8,128)} %copy-done.10, f32[2,256,256]{2,1,0:T(8,128)} %copy-done.1, f32[2,256,256]{2,1,0:T(8,128)} %copy-done.5), custom_call_target="tpu_custom_call" | custom-call | flops 4000000000 | bytes 4000000 | tf_op jit(solution)/shard_map/merge/pallas_call | solution.py:240
  90.4 0.0 copy-start.3
  90.4 11.3 %last.1 = (f32[256,256]{1,0:T(8,128)}, f32[256,256]{1,0:T(8,128)}) custom-call(s32[3,32]{1,0:T(4,128)} %rank_ref.13, f32[256,256]{1,0:T(8,128)} %merge.3.g_ref), custom_call_target="tpu_custom_call" | custom-call | flops 4000000000 | bytes 4000000 | tf_op jit(solution)/shard_map/last/pallas_call | solution.py:240
  101.7 0.0 collective-permute-start.4
  101.7 0.5 collective-permute-start.5
  102.2 0.0 copy-done.3
  102.2 1.8 %pad_maximum_fusion = f32[2,256,256]{2,1,0:T(8,128)} fusion(f32[1,256,256]{2,1,0:T(8,128)} %bitcast.11, f32[1,256,256]{2,1,0:T(8,128)S(1)} %bitcast.10), kind=kLoop, calls=%fused_computation | loop fusion | flops 131072 | bytes 1048576 | tf_op jit(solution)/shard_map/stack | solution.py:278
  104.0 0.0 collective-permute-done.6.co_ref
  104.0 0.0 copy-start.7
  104.0 0.0 collective-permute-done.4.lo_ref
  104.0 0.0 copy-start.8
  104.0 0.0 collective-permute-done.5.eo_ref
  104.1 0.7 copy-done.7
  104.7 0.1 copy-done.8
  104.8 0.0 copy-start.9
  104.8 0.7 copy-done.9
  105.5 13.5 %top.1 = f32[512,512]{1,0:T(8,128)} custom-call(s32[3,32]{1,0:T(4,128)} %rank_ref.13, f32[256,256]{1,0:T(8,128)} %get-tuple-element.5.l_ref, f32[256,256]{1,0:T(8,128)} %get-tuple-element.6.e_ref, f32[256,256]{1,0:T(8,128)} %copy-done.8, f32[256,256]{1,0:T(8,128)} %copy-done.9, f32[256,256]{1,0:T(8,128)} %copy-done.2, f32[256,256]{1,0:T(8,128)} %copy-done.7), custom_call_target="tpu_custom_call" | custom-call | flops 4000000000 | bytes 4000000 | tf_op jit(solution)/shard_map/top/pallas_call | solution.py:240
  (2 shorter events, 0.1 us)
Async XLA Ops:
  0.6 27.1 %copy-start.4 = (f32[1,2,256,256]{3,2,1,0:T(8,128)S(1)}, f32[1,2,256,256]{3,2,1,0:T(8,128)}, u32[]{:S(2)}) copy-start(f32[1,2,256,256]{3,2,1,0:T(8,128)} %param.7) | copy-start | bytes 1572868
  0.6 27.1 %copy-start = (f32[2,2,256,256]{3,2,1,0:T(8,128)S(1)}, f32[2,2,256,256]{3,2,1,0:T(8,128)}, u32[]{:S(2)}) copy-start(f32[2,2,256,256]{3,2,1,0:T(8,128)} %param.8) | copy-start | bytes 3145732
  24.8 16.9 %collective-permute-start = (f32[256,256]{1,0:T(8,128)}, f32[256,256]{1,0:T(8,128)}, u32[]{:S(2)}, u32[]{:S(2)}) collective-permute-start(f32[256,256]{1,0:T(8,128)} %leaf.1.g_ref), channel_id=1, source_target_pairs={{0,1},{1,0},{2,3},{3,2},{4,5},{5,4},{6,7},{7,6},{8,9},{9,8},{10,11... | collective-permute-start | bytes 786440 | tf_op jit(solution)/shard_map/ppermute | solution.py:252
  27.7 17.7 %collective-permute-start.1 = (f32[2,256,256]{2,1,0:T(8,128)S(1)}, f32[2,256,256]{2,1,0:T(8,128)S(1)}, u32[]{:S(2)}, u32[]{:S(2)}) collective-permute-start(f32[2,256,256]{2,1,0:T(8,128)S(1)} %bitcast.15), channel_id=1, source_target_pairs={{0,1},{1,0},{2,3},{3,2},{4,5},{5,4},{6,7},{7,6},{8,9},{9,8},{10,11... | collective-permute-start | bytes 1572872 | tf_op jit(solution)/shard_map/ppermute | solution.py:252
  27.8 13.8 %copy-start.1 = (f32[2,256,256]{2,1,0:T(8,128)}, f32[2,256,256]{2,1,0:T(8,128)S(1)}, u32[]{:S(2)}) copy-start(f32[2,256,256]{2,1,0:T(8,128)S(1)} %slice_bitcast_fusion.mine_ref) | copy-start | bytes 1572868
  27.8 46.3 %collective-permute-start.3 = (f32[2,256,256]{2,1,0:T(8,128)S(1)}, f32[2,256,256]{2,1,0:T(8,128)S(1)}, u32[]{:S(2)}, u32[]{:S(2)}) collective-permute-start(f32[2,256,256]{2,1,0:T(8,128)S(1)} %slice_bitcast_fusion.mine_ref), channel_id=1, source_target_pairs={{0,2},{1,3},{2,0},{3,1},{4,6},{5,7},{6,4},{7,5},{8,10},{9,11},{10,... | collective-permute-start | bytes 1572872 | tf_op jit(solution)/shard_map/ppermute | solution.py:252
  29.9 11.7 %copy-start.2 = (f32[256,256]{1,0:T(8,128)}, f32[256,256]{1,0:T(8,128)S(1)}, u32[]{:S(2)}) copy-start(f32[256,256]{1,0:T(8,128)S(1)} %slice_bitcast_fusion.1.c_ref) | copy-start | bytes 786436
  29.9 74.1 %collective-permute-start.6 = (f32[256,256]{1,0:T(8,128)S(1)}, f32[256,256]{1,0:T(8,128)S(1)}, u32[]{:S(2)}, u32[]{:S(2)}) collective-permute-start(f32[256,256]{1,0:T(8,128)S(1)} %slice_bitcast_fusion.1.c_ref), channel_id=1, source_target_pairs={{0,4},{4,0},{8,12},{12,8},{16,20},{20,16},{24,28},{28,24},{1,5},{5... | collective-permute-start | bytes 786440 | tf_op jit(solution)/shard_map/ppermute | solution.py:252
  45.5 0.8 copy-start.6
  60.9 13.2 %collective-permute-start.2 = (f32[256,256]{1,0:T(8,128)}, f32[256,256]{1,0:T(8,128)S(1)}, u32[]{:S(2)}, u32[]{:S(2)}) collective-permute-start(f32[256,256]{1,0:T(8,128)} %merge.2.g_ref), channel_id=1, source_target_pairs={{0,2},{1,3},{2,0},{3,1},{4,6},{5,7},{6,4},{7,5},{8,10},{9,11},{10,... | collective-permute-start | bytes 786440 | tf_op jit(solution)/shard_map/ppermute | solution.py:252
  74.1 0.8 copy-start.5
  74.9 0.7 copy-start.10
  90.4 11.9 %copy-start.3 = (f32[256,256]{1,0:T(8,128)S(1)}, f32[256,256]{1,0:T(8,128)}, u32[]{:S(2)}) copy-start(f32[256,256]{1,0:T(8,128)} %invert.3.l_ref) | copy-start | bytes 786436
  101.7 2.3 %collective-permute-start.4 = (f32[256,256]{1,0:T(8,128)}, f32[256,256]{1,0:T(8,128)S(1)}, u32[]{:S(2)}, u32[]{:S(2)}) collective-permute-start(f32[256,256]{1,0:T(8,128)} %get-tuple-element.5.l_ref), channel_id=1, source_target_pairs={{0,4},{4,0},{8,12},{12,8},{16,20},{20,16},{24,28},{28,24},{1,5},{5... | collective-permute-start | bytes 786440 | tf_op jit(solution)/shard_map/ppermute | solution.py:252
  101.7 2.3 %collective-permute-start.5 = (f32[256,256]{1,0:T(8,128)}, f32[256,256]{1,0:T(8,128)S(1)}, u32[]{:S(2)}, u32[]{:S(2)}) collective-permute-start(f32[256,256]{1,0:T(8,128)} %get-tuple-element.6.e_ref), channel_id=1, source_target_pairs={{0,4},{4,0},{8,12},{12,8},{16,20},{20,16},{24,28},{28,24},{1,5},{5... | collective-permute-start | bytes 786440 | tf_op jit(solution)/shard_map/ppermute | solution.py:252
  104.0 0.7 copy-start.7
  104.0 0.8 copy-start.8
  104.8 0.7 copy-start.9

commit v2 on v1

--- a/solution.py
+++ b/solution.py
@@ -113,26 +113,24 @@
             weights = []
             for t in range(tiles):
                 r1, r2, r3 = thirds(jnp.concatenate([rows[g][t] for g in range(groups)], axis=0))
-                above = jnp.zeros((q * PANEL, LANES), jnp.bfloat16)
-                below = jnp.zeros((LANES - (q + 1) * PANEL, LANES), jnp.bfloat16)
-
-                def tall(x, y):
-                    parts = [above, x, below, above, y, below]
-                    return jnp.concatenate([p for p in parts if p.shape[0]], axis=0)
-
-                weights.append((tall(r1, r1), tall(r2, r2), tall(r1, r3)))
+                blank = jnp.zeros((LANES - 2 * PANEL, LANES), jnp.bfloat16)
+                weights.append(jnp.concatenate([r1, r1, r2, r2, r1, r3, blank], axis=0))
 
             def updated(at, count):
                 inside = (wide[:count] >= q * PANEL) & (wide[:count] < (q + 1) * PANEL)
                 own = a_ref[pl.ds(at, count), pl.ds(own_at, LANES)]
-                l1, l2, l3 = thirds(jnp.where(inside, own, 0.0))
-                l12 = jnp.concatenate([l1, l2], axis=1)
-                l31 = jnp.concatenate([l3, l1], axis=1)
                 olds = [jnp.where(inside, 0.0, own)] + [a_ref[pl.ds(at, count), pl.ds(spot, LANES)] for spot in spots[1:]]
-                return [
-                    old - (bdot(l12, w11) + (bdot(l12, w22) + bdot(l31, w13)))
-                    for old, (w11, w22, w13) in zip(olds, weights)
-                ]
+                x = jnp.where(inside, own, 0.0)
+                x = x + pltpu.roll(x, PANEL, 1)
+                x = x + pltpu.roll(x, 2 * PANEL, 1)
+                l1 = x.astype(jnp.bfloat16).astype(jnp.float32)
+                l2 = (x - l1).astype(jnp.bfloat16).astype(jnp.float32)
+                l3 = x - l1 - l2
+                at_quarter = wide[:count] // PANEL
+                one = jnp.where((at_quarter & 1) == 0, l1, l2)
+                two = jnp.where(at_quarter == 0, l3, jnp.where(at_quarter == 1, l1, 0.0))
+                lhs = jnp.concatenate([one.astype(jnp.bfloat16), two.astype(jnp.bfloat16)], axis=1)
+                return [old - bdot(lhs, w) for old, w in zip(olds, weights)]
 
             ahead = None
             if q != panels[-1]:

time: 119 us -> 119 us (level)
  transfers between devices with their start and end apart: 7 -> 7, of which waited for: 1 -> 1; matrix products, arithmetic and copies ran while one was open for 2% -> 2% of each run, Pallas kernels for 54% -> 53%
where the time goes in v2:
time: 119 us; the launch traced here: 118 us
  Pallas kernels  101 us (85%)
  starting transfers between devices  7.44 us (6%)
  waiting for transfers between devices  4.08 us (3%)
  local copies, waits for them, and re-layouts  3.84 us (3%)
  other arithmetic  1.78 us (1%)
    pallas_call x7, Pallas kernels, call(): pl.pallas_call(kernel, name=name, out_shape=[jax.ShapeDtypeStruct(shape,...  101 us
    ppermute x7, starting transfers between devices, partner(): lax.ppermute(x, axis, [(i, i ^ 1 << bit) for i in range(lax.axis_size(axi...  7.44 us
    ppermute x7, waiting for transfers between devices, partner(): lax.ppermute(x, axis, [(i, i ^ 1 << bit) for i in range(lax.axis_size(axi...  4.08 us
    unnamed x22, local copies, waits for them, and re-layouts  3.79 us
  transfers between devices with their start and end apart: 7, of which 1 were waited for; matrix products, arithmetic and copies ran while one was open for 2% of the time, Pallas kernels for 53%

profile of v2, /device:TPU:0, one launch (start us, length us, event | category | flops | bytes accessed | tf_op | source)
XLA Modules:
  0.0 118.4 jit_solution(14497284160647017352)
XLA Ops:
  0.6 0.0 copy-start.4
  0.6 0.0 copy-start
  0.7 24.0 %leaf.1.g_ref = f32[256,256]{1,0:T(8,128)} custom-call(s32[3,32]{1,0:T(4,128)} %rank_ref.13, f32[512,512]{1,0:T(8,128)} %bitcast.12, f32[512,256]{1,0:T(8,128)} %bitcast.13), custom_call_target="tpu_custom_call" | custom-call | flops 4000000000 | bytes 4000000 | tf_op jit(solution)/shard_map/leaf/pallas_call | solution.py:238
  24.7 3.0 %collective-permute-start = (f32[256,256]{1,0:T(8,128)}, f32[256,256]{1,0:T(8,128)}, u32[]{:S(2)}, u32[]{:S(2)}) collective-permute-start(f32[256,256]{1,0:T(8,128)} %leaf.1.g_ref), channel_id=1, source_target_pairs={{0,1},{1,0},{2,3},{3,2},{4,5},{5,4},{6,7},{7,6},{8,9},{9,8},{10,11... | collective-permute-start | bytes 786440 | tf_op jit(solution)/shard_map/ppermute | solution.py:250
  27.6 0.0 copy-done.4
  27.6 0.0 collective-permute-start.1
  27.6 0.0 copy-done
  27.7 0.0 copy-start.1
  27.7 2.1 %collective-permute-start.3 = (f32[2,256,256]{2,1,0:T(8,128)S(1)}, f32[2,256,256]{2,1,0:T(8,128)S(1)}, u32[]{:S(2)}, u32[]{:S(2)}) collective-permute-start(f32[2,256,256]{2,1,0:T(8,128)S(1)} %slice_bitcast_fusion.mine_ref), channel_id=1, source_target_pairs={{0,2},{1,3},{2,0},{3,1},{4,6},{5,7},{6,4},{7,5},{8,10},{9,11},{10,... | collective-permute-start | bytes 1572872 | tf_op jit(solution)/shard_map/ppermute | solution.py:250
  29.8 0.0 copy-start.2
  29.8 0.1 collective-permute-start.6
  29.9 11.4 %invert.2.l_ref = f32[256,256]{1,0:T(8,128)} custom-call(s32[3,32]{1,0:T(4,128)} %rank_ref.13, f32[256,256]{1,0:T(8,128)} %leaf.1.g_ref), custom_call_target="tpu_custom_call" | custom-call | flops 4000000000 | bytes 4000000 | tf_op jit(solution)/shard_map/invert/pallas_call | solution.py:238
  41.3 0.0 copy-done.1
  41.3 0.0 copy-done.2
  41.3 0.0 collective-permute-done.gy_ref
  41.3 4.1 %collective-permute-done.1.theirs_ref = f32[2,256,256]{2,1,0:T(8,128)S(1)} collective-permute-done((f32[2,256,256]{2,1,0:T(8,128)S(1)}, f32[2,256,256]{2,1,0:T(8,128)S(1)}, u32[]{:S(2)}, u32[]{:S(2)}) %collective-permute-start.1) | collective-permute-done | bytes 524320 | tf_op jit(solution)/shard_map/ppermute | solution.py:250
  45.4 0.0 copy-start.6
  45.4 0.8 copy-done.6
  46.2 14.7 %merge.2.g_ref = f32[256,256]{1,0:T(8,128)} custom-call(s32[3,32]{1,0:T(4,128)} %rank_ref.13, f32[256,256]{1,0:T(8,128)} %invert.2.l_ref, f32[256,256]{1,0:T(8,128)} %collective-permute-done.gy_ref, f32[2,256,256]{2,1,0:T(8,128)} %bitcast.14, f32[2,256,256]{2,1,0:T(8,128)} %copy-done.6), custom_call_target="tpu_custom_call" | custom-call | flops 4000000000 | bytes 4000000 | tf_op jit(solution)/shard_map/merge/pallas_call | solution.py:238
  60.9 1.8 %collective-permute-start.2 = (f32[256,256]{1,0:T(8,128)}, f32[256,256]{1,0:T(8,128)S(1)}, u32[]{:S(2)}, u32[]{:S(2)}) collective-permute-start(f32[256,256]{1,0:T(8,128)} %merge.2.g_ref), channel_id=1, source_target_pairs={{0,2},{1,3},{2,0},{3,1},{4,6},{5,7},{6,4},{7,5},{8,10},{9,11},{10,... | collective-permute-start | bytes 786440 | tf_op jit(solution)/shard_map/ppermute | solution.py:250
  62.6 11.4 %invert.3.l_ref = f32[256,256]{1,0:T(8,128)} custom-call(s32[3,32]{1,0:T(4,128)} %rank_ref.13, f32[256,256]{1,0:T(8,128)} %merge.2.g_ref), custom_call_target="tpu_custom_call" | custom-call | flops 4000000000 | bytes 4000000 | tf_op jit(solution)/shard_map/invert/pallas_call | solution.py:238
  74.0 0.0 collective-permute-done.3.theirs_ref
  74.0 0.0 copy-start.5
  74.0 0.0 collective-permute-done.2.gy_ref
  74.1 0.8 copy-done.5
  74.8 0.0 copy-start.10
  74.8 0.7 copy-done.10
  75.5 14.5 %merge.3.g_ref = f32[256,256]{1,0:T(8,128)} custom-call(s32[3,32]{1,0:T(4,128)} %rank_ref.13, f32[256,256]{1,0:T(8,128)} %invert.3.l_ref, f32[256,256]{1,0:T(8,128)} %copy-done.10, f32[2,256,256]{2,1,0:T(8,128)} %copy-done.1, f32[2,256,256]{2,1,0:T(8,128)} %copy-done.5), custom_call_target="tpu_custom_call" | custom-call | flops 4000000000 | bytes 4000000 | tf_op jit(solution)/shard_map/merge/pallas_call | solution.py:238
  90.1 0.0 copy-start.3
  90.1 11.2 %last.1 = (f32[256,256]{1,0:T(8,128)}, f32[256,256]{1,0:T(8,128)}) custom-call(s32[3,32]{1,0:T(4,128)} %rank_ref.13, f32[256,256]{1,0:T(8,128)} %merge.3.g_ref), custom_call_target="tpu_custom_call" | custom-call | flops 4000000000 | bytes 4000000 | tf_op jit(solution)/shard_map/last/pallas_call | solution.py:238
  101.2 0.0 collective-permute-start.4
  101.2 0.5 collective-permute-start.5
  101.8 0.0 copy-done.3
  101.8 1.8 %pad_maximum_fusion = f32[2,256,256]{2,1,0:T(8,128)} fusion(f32[1,256,256]{2,1,0:T(8,128)} %bitcast.11, f32[1,256,256]{2,1,0:T(8,128)S(1)} %bitcast.10), kind=kLoop, calls=%fused_computation | loop fusion | flops 131072 | bytes 1048576 | tf_op jit(solution)/shard_map/stack | solution.py:276
  103.5 0.0 collective-permute-done.6.co_ref
  103.5 0.0 copy-start.7
  103.5 0.0 collective-permute-done.4.lo_ref
  103.5 0.0 copy-start.8
  103.6 0.0 collective-permute-done.5.eo_ref
  103.6 0.7 copy-done.7
  104.2 0.1 copy-done.8
  104.3 0.0 copy-start.9
  104.3 0.7 copy-done.9
  105.0 13.4 %top.1 = f32[512,512]{1,0:T(8,128)} custom-call(s32[3,32]{1,0:T(4,128)} %rank_ref.13, f32[256,256]{1,0:T(8,128)} %get-tuple-element.5.l_ref, f32[256,256]{1,0:T(8,128)} %get-tuple-element.6.e_ref, f32[256,256]{1,0:T(8,128)} %copy-done.8, f32[256,256]{1,0:T(8,128)} %copy-done.9, f32[256,256]{1,0:T(8,128)} %copy-done.2, f32[256,256]{1,0:T(8,128)} %copy-done.7), custom_call_target="tpu_custom_call" | custom-call | flops 4000000000 | bytes 4000000 | tf_op jit(solution)/shard_map/top/pallas_call | solution.py:238
  (2 shorter events, 0.1 us)
Async XLA Ops:
  0.6 27.0 %copy-start.4 = (f32[1,2,256,256]{3,2,1,0:T(8,128)S(1)}, f32[1,2,256,256]{3,2,1,0:T(8,128)}, u32[]{:S(2)}) copy-start(f32[1,2,256,256]{3,2,1,0:T(8,128)} %param.7) | copy-start | bytes 1572868
  0.6 27.0 %copy-start = (f32[2,2,256,256]{3,2,1,0:T(8,128)S(1)}, f32[2,2,256,256]{3,2,1,0:T(8,128)}, u32[]{:S(2)}) copy-start(f32[2,2,256,256]{3,2,1,0:T(8,128)} %param.8) | copy-start | bytes 3145732
  24.7 16.6 %collective-permute-start = (f32[256,256]{1,0:T(8,128)}, f32[256,256]{1,0:T(8,128)}, u32[]{:S(2)}, u32[]{:S(2)}) collective-permute-start(f32[256,256]{1,0:T(8,128)} %leaf.1.g_ref), channel_id=1, source_target_pairs={{0,1},{1,0},{2,3},{3,2},{4,5},{5,4},{6,7},{7,6},{8,9},{9,8},{10,11... | collective-permute-start | bytes 786440 | tf_op jit(solution)/shard_map/ppermute | solution.py:250
  27.6 17.7 %collective-permute-start.1 = (f32[2,256,256]{2,1,0:T(8,128)S(1)}, f32[2,256,256]{2,1,0:T(8,128)S(1)}, u32[]{:S(2)}, u32[]{:S(2)}) collective-permute-start(f32[2,256,256]{2,1,0:T(8,128)S(1)} %bitcast.15), channel_id=1, source_target_pairs={{0,1},{1,0},{2,3},{3,2},{4,5},{5,4},{6,7},{7,6},{8,9},{9,8},{10,11... | collective-permute-start | bytes 1572872 | tf_op jit(solution)/shard_map/ppermute | solution.py:250
  27.7 13.6 %copy-start.1 = (f32[2,256,256]{2,1,0:T(8,128)}, f32[2,256,256]{2,1,0:T(8,128)S(1)}, u32[]{:S(2)}) copy-start(f32[2,256,256]{2,1,0:T(8,128)S(1)} %slice_bitcast_fusion.mine_ref) | copy-start | bytes 1572868
  27.7 46.4 %collective-permute-start.3 = (f32[2,256,256]{2,1,0:T(8,128)S(1)}, f32[2,256,256]{2,1,0:T(8,128)S(1)}, u32[]{:S(2)}, u32[]{:S(2)}) collective-permute-start(f32[2,256,256]{2,1,0:T(8,128)S(1)} %slice_bitcast_fusion.mine_ref), channel_id=1, source_target_pairs={{0,2},{1,3},{2,0},{3,1},{4,6},{5,7},{6,4},{7,5},{8,10},{9,11},{10,... | collective-permute-start | bytes 1572872 | tf_op jit(solution)/shard_map/ppermute | solution.py:250
  29.8 11.5 %copy-start.2 = (f32[256,256]{1,0:T(8,128)}, f32[256,256]{1,0:T(8,128)S(1)}, u32[]{:S(2)}) copy-start(f32[256,256]{1,0:T(8,128)S(1)} %slice_bitcast_fusion.1.c_ref) | copy-start | bytes 786436
  29.8 73.7 %collective-permute-start.6 = (f32[256,256]{1,0:T(8,128)S(1)}, f32[256,256]{1,0:T(8,128)S(1)}, u32[]{:S(2)}, u32[]{:S(2)}) collective-permute-start(f32[256,256]{1,0:T(8,128)S(1)} %slice_bitcast_fusion.1.c_ref), channel_id=1, source_target_pairs={{0,4},{4,0},{8,12},{12,8},{16,20},{20,16},{24,28},{28,24},{1,5},{5... | collective-permute-start | bytes 786440 | tf_op jit(solution)/shard_map/ppermute | solution.py:250
  45.4 0.8 copy-start.6
  60.9 13.2 %collective-permute-start.2 = (f32[256,256]{1,0:T(8,128)}, f32[256,256]{1,0:T(8,128)S(1)}, u32[]{:S(2)}, u32[]{:S(2)}) collective-permute-start(f32[256,256]{1,0:T(8,128)} %merge.2.g_ref), channel_id=1, source_target_pairs={{0,2},{1,3},{2,0},{3,1},{4,6},{5,7},{6,4},{7,5},{8,10},{9,11},{10,... | collective-permute-start | bytes 786440 | tf_op jit(solution)/shard_map/ppermute | solution.py:250
  74.0 0.8 copy-start.5
  74.8 0.7 copy-start.10
  90.1 11.7 %copy-start.3 = (f32[256,256]{1,0:T(8,128)S(1)}, f32[256,256]{1,0:T(8,128)}, u32[]{:S(2)}) copy-start(f32[256,256]{1,0:T(8,128)} %invert.3.l_ref) | copy-start | bytes 786436
  101.2 2.3 %collective-permute-start.4 = (f32[256,256]{1,0:T(8,128)}, f32[256,256]{1,0:T(8,128)S(1)}, u32[]{:S(2)}, u32[]{:S(2)}) collective-permute-start(f32[256,256]{1,0:T(8,128)} %get-tuple-element.5.l_ref), channel_id=1, source_target_pairs={{0,4},{4,0},{8,12},{12,8},{16,20},{20,16},{24,28},{28,24},{1,5},{5... | collective-permute-start | bytes 786440 | tf_op jit(solution)/shard_map/ppermute | solution.py:250
  101.2 2.3 %collective-permute-start.5 = (f32[256,256]{1,0:T(8,128)}, f32[256,256]{1,0:T(8,128)S(1)}, u32[]{:S(2)}, u32[]{:S(2)}) collective-permute-start(f32[256,256]{1,0:T(8,128)} %get-tuple-element.6.e_ref), channel_id=1, source_target_pairs={{0,4},{4,0},{8,12},{12,8},{16,20},{20,16},{24,28},{28,24},{1,5},{5... | collective-permute-start | bytes 786440 | tf_op jit(solution)/shard_map/ppermute | solution.py:250
  103.5 0.7 copy-start.7
  103.5 0.8 copy-start.8
  104.3 0.7 copy-start.9
